TPU v7x, 512 devices: a whole 4x4x16 slice. The times are simulated.
512 devices in a mesh: row: 16 (over y, x), col: 32 (over z, core).
Axes of the slice: x: 4, y: 4, z: 16, core: 2. Of those that a mesh axis runs over, the one named last changes fastest.
Arguments:
- root_inverse: bfloat16 [4096, 4096], P('row', 'col'), may hold values from -16 to 16
- factor: bfloat16 [4096, 4, 4096], P('row', None, 'col'), may hold values from -0.59765625 to 0.59765625
- inverse_diag: bfloat16 [4096, 4, 4096], P('row', None, 'col'), may hold values from -6 to 6
- structure: int32 [4, 32], replicated, may hold values 0 or 1
Outputs:
- ainv_rk: bfloat16 [4096, 4, 4096], P('row', None, 'col')
- ainv_kk: bfloat16 [4096, 4, 4096], P('row', None, 'col')
All inputs are finite; a program needn't handle non-finite values.
Results may differ from a plain program's by a relative error of at most 0.014.
Values may be sent and summed in bfloat16 or wider, within the bound.
No kernel may reach another device: no remote copies, remote signals or barrier semaphores. Data moves between devices by JAX's collectives and lax.ppermute only.
A program may use at most 64 MiB of HBM per device.

v0:
```python
import jax
import jax.numpy as jnp
from jax import lax
from jax.sharding import PartitionSpec as P

BLK = 128


def body(root_inverse, factor, inverse_diag, structure):
    local_rows = factor.shape[0]
    offset = lax.axis_index("row") * local_rows
    row_mask = jnp.repeat(structure, BLK, axis=1)
    local_mask = lax.dynamic_slice_in_dim(row_mask, offset, local_rows, 1).T.astype(factor.dtype)
    masked = factor * local_mask[:, :, None]
    root_rows = lax.all_gather(root_inverse, "col", axis=1, tiled=True)
    product = jnp.einsum(
        "ik,knj->inj",
        root_rows,
        lax.all_gather(masked, "row", axis=0, tiled=True),
        preferred_element_type=jnp.float32,
    )
    ainv_rk = (-product).astype(jnp.bfloat16)
    inverse_rows = lax.all_gather(ainv_rk, "col", axis=2, tiled=True)
    running = lax.psum_scatter(
        jnp.einsum("kni,knj->inj", inverse_rows, masked, preferred_element_type=jnp.float32).astype(
            jnp.bfloat16
        ),
        "row",
        scatter_dimension=0,
        tiled=True,
    ).astype(jnp.float32)
    ainv_kk = (inverse_diag.astype(jnp.float32) - running).astype(jnp.bfloat16)
    return (ainv_rk, ainv_kk)


def solution(mesh):
    return jax.shard_map(
        body,
        mesh=mesh,
        in_specs=(P("row", "col"), P("row", None, "col"), P("row", None, "col"), P()),
        out_specs=(P("row", None, "col"), P("row", None, "col")),
        check_vma=False,
    )
```

profile of v0, /device:TPU:32, one launch (start us, length us, event | category | flops | bytes accessed | tf_op | source)
XLA Modules:
  0.0 349.0 jit_solution(17044077061663513549)
XLA Ops:
  7.2 0.0 copy-start
  7.2 0.0 all-gather.6.cloned.1.call-start
  7.2 0.7 all-gather.6.cloned.1.call-update
  7.9 0.0 all-gather.4.cloned.1.call-start
  8.0 0.1 broadcast_bitcast_fusion
  8.0 0.1 copy.14
  8.1 1.1 copy.6
  9.2 0.7 broadcast_multiply_fusion
  10.0 0.0 all-gather.4.cloned.1.call-update
  10.0 0.0 all-gather.8.cloned.1.call-start
  10.0 76.9 %all-gather.6.cloned.1.call-done = bf16[256,4096]{1,0:T(8,128)(2,1)} async-done(((bf16[256,128]{1,0:T(8,128)(2,1)}), bf16[256,4096]{1,0:T(8,128)(2,1)}) %all-gather.6.cloned.1.call-update) | async-done | bytes 2097168 | tf_op jit(solution)/shard_map/all_gather | solution.py:15
  86.9 71.7 %all-gather.4.cloned.1.call-done = bf16[4096,4,128]{0,2,1:T(8,128)(2,1)} async-done(((bf16[256,4,128]{0,2,1:T(8,128)(2,1)}), bf16[4096,4,128]{0,2,1:T(8,128)(2,1)}) %all-gather.4.cloned.1.call-update) | async-done | bytes 4194320 | tf_op jit(solution)/shard_map/all_gather | solution.py:19
  158.6 4.9 %fusion.9 = bf16[256,4,128]{0,2,1:T(8,128)(2,1)} fusion(bf16[4096,4,128]{0,2,1:T(8,128)(2,1)} %all-gather.4.cloned.1.call-done, bf16[256,4096]{1,0:T(8,128)(2,1)} %all-gather.6.cloned.1.call-done), kind=kOutput, calls=%fused_computation.6 | convolution fusion | flops 1074003968 | bytes 6553600 | tf_op jit(solution)/shard_map/ik,knj->inj/dot_general | solution.py:16
  163.5 0.0 all-gather.8.cloned.1.call-update
  163.5 0.0 reduce-scatter.2.cloned.1.call-start
  163.5 78.3 %all-gather.8.cloned.1.call-done = bf16[256,4,4096]{0,2,1:T(8,128)(2,1)} async-done(((bf16[256,4,128]{0,2,1:T(8,128)(2,1)}), bf16[256,4,4096]{0,2,1:T(8,128)(2,1)}) %all-gather.8.cloned.1.call-update) | async-done | bytes 8388624 | tf_op jit(solution)/shard_map/all_gather | solution.py:23
  241.9 8.2 %fusion = bf16[4096,4,128]{0,2,1:T(8,128)(2,1)} fusion(bf16[256,4,128]{0,2,1:T(8,128)(2,1)S(1)} %copy-done.1, bf16[256,4,4096]{0,2,1:T(8,128)(2,1)} %all-gather.8.cloned.1.call-done), kind=kOutput, calls=%fused_computation.1 | convolution fusion | flops 1075838976 | bytes 12845056 | tf_op jit(solution)/shard_map/kni,knj->inj/dot_general | solution.py:25
  250.1 0.0 reduce-scatter.2.cloned.1.call-update
  250.1 0.9 copy-done.3
  251.0 0.2 copy.7
  251.2 0.9 copy.9
  252.1 88.5 %reduce-scatter.2.cloned.1.call-done = bf16[256,4,128]{0,2,1:T(8,128)(2,1)} async-done(((bf16[4096,4,128]{0,2,1:T(8,128)(2,1)}), bf16[256,4,128]{0,2,1:T(8,128)(2,1)}) %reduce-scatter.2.cloned.1.call-update) | async-done | bytes 262160 | tf_op jit(solution)/shard_map/reduce_scatter | solution.py:24
  340.6 1.0 subtract_convert_fusion
  341.6 0.9 copy.10
  (7 shorter events, 0.0 us)
Async XLA Ops:
  7.2 0.8 copy-start
  7.2 79.7 %all-gather.6.cloned.1.call-start = ((), (), s32[]{:S(2)}) async-start(), calls=%async_computation.2 | async-start | bytes 2162688 | tf_op jit(solution)/shard_map/all_gather | solution.py:15
  7.9 150.7 %all-gather.4.cloned.1.call-start = ((), (), s32[]{:S(2)}) async-start(), calls=%async_computation.1 | async-start | bytes 4456448 | tf_op jit(solution)/shard_map/all_gather | solution.py:19
  10.0 231.9 %copy-start.1 = (bf16[256,4,128]{0,2,1:T(8,128)(2,1)S(1)}, bf16[256,4,128]{0,2,1:T(8,128)(2,1)}, u32[]{:S(2)}) copy-start(bf16[256,4,128]{0,2,1:T(8,128)(2,1)} %broadcast_multiply_fusion) | copy-start | bytes 786436
  10.0 231.9 %all-gather.8.cloned.1.call-start = ((), (), s32[]{:S(2)}) async-start(), calls=%async_computation.3 | async-start | bytes 8650752 | tf_op jit(solution)/shard_map/all_gather | solution.py:23
  163.5 177.1 %reduce-scatter.2.cloned.1.call-start = ((), (), s32[]{:S(2)}) async-start(), calls=%async_computation.4 | async-start | bytes 4456448 | tf_op jit(solution)/shard_map/reduce_scatter | solution.py:24
  250.1 0.9 copy-start.3
  250.1 1.1 copy-start.2
Sparse Core Ops, SparseCore 0:
  10.0 76.8 all-gather.5
  90.5 68.0 all-gather.3
  163.6 78.2 all-gather.7
  250.2 90.3 reduce-scatter.1
where the time goes:
time: 349 us
  waiting for transfers between devices  316 us (91%)
  between operations  13.8 us (4%)
  matrix products  13 us (4%)
  local copies, waits for them, and re-layouts  4.08 us (1%)
    reduce_scatter x1, waiting for transfers between devices, body(): lax.psum_scatter(jnp.einsum('kni,knj->inj', inverse_rows, masked, preferr...  88.5 us
    all_gather x1, waiting for transfers between devices, body(): inverse_rows = lax.all_gather(ainv_rk, 'col', axis=2, tiled=True)  78.3 us
    all_gather x1, waiting for transfers between devices, body(): root_rows = lax.all_gather(root_inverse, 'col', axis=1, tiled=True)  76.9 us
    all_gather x1, waiting for transfers between devices, body(): lax.all_gather(masked, 'row', axis=0, tiled=True)  71.7 us
    dot_general x1, matrix products, body(): jnp.einsum('kni,knj->inj', inverse_rows, masked, preferred_element_type=j...  8.19 us
  transfers between devices with their start and end apart: 4, of which 4 were waited for; matrix products, arithmetic and copies ran while one was open for 1% of the time, Pallas kernels for 0%

commit v1 on v0

--- a/solution.py
+++ b/solution.py
@@ -12,7 +12,10 @@
     row_mask = jnp.repeat(structure, BLK, axis=1)
     local_mask = lax.dynamic_slice_in_dim(row_mask, offset, local_rows, 1).T.astype(factor.dtype)
     masked = factor * local_mask[:, :, None]
-    root_rows = lax.all_gather(root_inverse, "col", axis=1, tiled=True)
+    size = lax.axis_size("col")
+    pieces = jnp.stack([root_inverse for _ in range(size)])
+    pieces = lax.all_to_all(pieces, "col", split_axis=0, concat_axis=0)
+    root_rows = jnp.concatenate(pieces, axis=1)
     product = jnp.einsum(
         "ik,knj->inj",
         root_rows,

time: 349 us -> 314 us (0.90)
  waiting for transfers between devices: 316 us -> 259 us
  starting transfers between devices: 0.16 us -> 15.5 us
  local copies, waits for them, and re-layouts: 4.08 us -> 11.4 us
    all_to_all x0 -> x1, waiting for transfers between devices: none -> 98.9 us  [body(): pieces = lax.all_to_all(pieces, 'col', split_axis=0, concat_axis=0)]
    all_gather x1 -> x0, waiting for transfers between devices: 76.9 us -> none  [body(): root_rows = lax.all_gather(root_inverse, 'col', axis=1, tiled=True)]
    all_gather x1, waiting for transfers between devices: 71.7 us -> 0.02 us  [body(): lax.all_gather(masked, 'row', axis=0, tiled=True)]
    all_to_all x0 -> x1, starting transfers between devices: none -> 15.4 us  [body(): pieces = lax.all_to_all(pieces, 'col', split_axis=0, concat_axis=0)]
    all_gather x1, waiting for transfers between devices: 78.3 us -> 71.3 us  [body(): inverse_rows = lax.all_gather(ainv_rk, 'col', axis=2, tiled=True)]
    reshape x0 -> x2, local copies, waits for them, and re-layouts: none -> 5.51 us  [body(): root_rows = jnp.concatenate(pieces, axis=1)]
  transfers between devices with their start and end apart: 4 -> 4, of which waited for: 4 -> 3; matrix products, arithmetic and copies ran while one was open for 1% -> 2% of each run, Pallas kernels for 0% -> 0%
where the time goes in v1:
time: 314 us
  waiting for transfers between devices  259 us (82%)
  starting transfers between devices  15.5 us (5%)
  between operations  13.9 us (4%)
  matrix products  12.4 us (4%)
  local copies, waits for them, and re-layouts  11.4 us (4%)
    all_to_all x1, waiting for transfers between devices, body(): pieces = lax.all_to_all(pieces, 'col', split_axis=0, concat_axis=0)  98.9 us
    reduce_scatter x1, waiting for transfers between devices, body(): lax.psum_scatter(jnp.einsum('kni,knj->inj', inverse_rows, masked, preferr...  88.5 us
    all_gather x1, waiting for transfers between devices, body(): inverse_rows = lax.all_gather(ainv_rk, 'col', axis=2, tiled=True)  71.3 us
    all_to_all x1, starting transfers between devices, body(): pieces = lax.all_to_all(pieces, 'col', split_axis=0, concat_axis=0)  15.4 us
    dot_general x1, matrix products, body(): jnp.einsum('kni,knj->inj', inverse_rows, masked, preferred_element_type=j...  8.18 us
  transfers between devices with their start and end apart: 4, of which 3 were waited for; matrix products, arithmetic and copies ran while one was open for 2% of the time, Pallas kernels for 0%

profile of v1, /device:TPU:32, one launch (start us, length us, event | category | flops | bytes accessed | tf_op | source)
XLA Modules:
  0.0 313.6 jit_solution(11268897736941292034)
XLA Ops:
  7.2 2.7 stack.2
  9.9 15.4 %all-to-all-start = ((bf16[32,256,128]{2,1,0:T(8,128)(2,1)}), bf16[32,256,128]{2,1,0:T(8,128)(2,1)S(1)}, u32[]{:S(2)}, u32[]{:S(2)}) async-start(bf16[32,256,128]{2,1,0:T(8,128)(2,1)} %stack.2), calls=%async_computation | async-start | bytes 4194304 | tf_op jit(solution)/shard_map/all_to_all | solution.py:17
  25.2 0.0 all-gather.3.cloned.1.call-start
  25.3 0.1 broadcast_bitcast_fusion
  25.4 0.1 copy.20
  25.5 0.2 copy.11
  25.6 0.7 broadcast_multiply_fusion
  26.4 0.0 all-gather.3.cloned.1.call-update
  26.4 0.0 all-gather.5.cloned.1.call-start
  26.4 98.9 %all-to-all-done = bf16[32,256,128]{2,1,0:T(8,128)(2,1)S(1)} async-done(((bf16[32,256,128]{2,1,0:T(8,128)(2,1)}), bf16[32,256,128]{2,1,0:T(8,128)(2,1)S(1)}, u32[]{:S(2)}, u32[]{:S(2)}) %all-to-all-start) | async-done | bytes 2097184 | tf_op jit(solution)/shard_map/all_to_all | solution.py:17
  125.3 2.7 copy.12
  128.0 2.8 reshape.19
  130.8 0.0 all-gather.3.cloned.1.call-done
  130.9 4.2 %fusion.2 = bf16[256,4,128]{0,2,1:T(8,128)(2,1)} fusion(bf16[4096,4,128]{0,2,1:T(8,128)(2,1)} %all-gather.3.cloned.1.call-done, bf16[256,4096,1]{1,0,2:T(8,128)(2,1)S(1)} %reshape.19), kind=kOutput, calls=%fused_computation.4 | convolution fusion | flops 1074003968 | bytes 6553600 | tf_op jit(solution)/shard_map/ik,knj->inj/dot_general | solution.py:19
  135.1 0.0 all-gather.5.cloned.1.call-update
  135.1 0.0 reduce-scatter.2.cloned.1.call-start
  135.2 71.3 %all-gather.5.cloned.1.call-done = bf16[256,4,4096]{0,2,1:T(8,128)(2,1)} async-done(((bf16[256,4,128]{0,2,1:T(8,128)(2,1)}), bf16[256,4,4096]{0,2,1:T(8,128)(2,1)}) %all-gather.5.cloned.1.call-update) | async-done | bytes 8388624 | tf_op jit(solution)/shard_map/all_gather | solution.py:26
  206.5 8.2 %fusion = bf16[4096,4,128]{0,2,1:T(8,128)(2,1)} fusion(bf16[256,4,128]{0,2,1:T(8,128)(2,1)S(1)} %copy-done.1, bf16[256,4,4096]{0,2,1:T(8,128)(2,1)} %all-gather.5.cloned.1.call-done), kind=kOutput, calls=%fused_computation.1 | convolution fusion | flops 1075838976 | bytes 12845056 | tf_op jit(solution)/shard_map/kni,knj->inj/dot_general | solution.py:28
  214.7 0.9 copy-done.4
  215.6 0.2 copy.13
  215.8 0.9 copy.15
  216.7 88.5 %reduce-scatter.2.cloned.1.call-done = bf16[256,4,128]{0,2,1:T(8,128)(2,1)} async-done(((bf16[4096,4,128]{0,2,1:T(8,128)(2,1)}), bf16[256,4,128]{0,2,1:T(8,128)(2,1)}) %reduce-scatter.2.cloned.1.call-update) | async-done | bytes 262160 | tf_op jit(solution)/shard_map/reduce_scatter | solution.py:27
  305.1 1.0 subtract_convert_fusion
  306.2 0.9 copy.16
  (11 shorter events, 0.1 us)
Async XLA Ops:
  7.2 18.1 %copy-start = (s32[4,32]{1,0:T(4,128)S(1)}, s32[4,32]{1,0:T(4,128)}, u32[]{:S(2)}) copy-start(s32[4,32]{1,0:T(4,128)} %param.7) | copy-start | bytes 1540
  7.2 18.3 %copy-start.3 = (bf16[256,4,128]{2,1,0:T(4,128)(2,1)S(1)}, bf16[256,4,128]{2,1,0:T(4,128)(2,1)}, u32[]{:S(2)}) copy-start(bf16[256,4,128]{2,1,0:T(4,128)(2,1)} %param.5) | copy-start | bytes 786436
  9.9 115.4 %all-to-all-start = ((bf16[32,256,128]{2,1,0:T(8,128)(2,1)}), bf16[32,256,128]{2,1,0:T(8,128)(2,1)S(1)}, u32[]{:S(2)}, u32[]{:S(2)}) async-start(bf16[32,256,128]{2,1,0:T(8,128)(2,1)} %stack.2), calls=%async_computation | async-start | bytes 4194304 | tf_op jit(solution)/shard_map/all_to_all | solution.py:17
  25.2 105.6 %all-gather.3.cloned.1.call-start = ((), (), s32[]{:S(2)}) async-start(), calls=%async_computation.2 | async-start | bytes 4456448 | tf_op jit(solution)/shard_map/all_gather | solution.py:22
  26.4 180.1 %all-gather.5.cloned.1.call-start = ((), (), s32[]{:S(2)}) async-start(), calls=%async_computation.3 | async-start | bytes 8650752 | tf_op jit(solution)/shard_map/all_gather | solution.py:26
  130.8 75.6 %copy-start.1 = (bf16[256,4,128]{0,2,1:T(8,128)(2,1)S(1)}, bf16[256,4,128]{0,2,1:T(8,128)(2,1)}, u32[]{:S(2)}) copy-start(bf16[256,4,128]{0,2,1:T(8,128)(2,1)} %broadcast_multiply_fusion) | copy-start | bytes 786436
  135.1 170.0 %reduce-scatter.2.cloned.1.call-start = ((), (), s32[]{:S(2)}) async-start(), calls=%async_computation.4 | async-start | bytes 4456448 | tf_op jit(solution)/shard_map/reduce_scatter | solution.py:27
  214.6 0.9 copy-start.4
  214.6 1.1 copy-start.2
Sparse Core Ops, SparseCore 0:
  29.6 73.0 all-gather.2
  135.2 71.1 all-gather.4
  214.8 90.3 reduce-scatter.1
